TPU v7x, 32 devices: a whole 2x2x4 slice. The times are simulated.
32 devices in a mesh: seg: 8 (over y, x, core), slab: 4 (over z).
Axes of the slice: x: 2, y: 2, z: 4, core: 2. Of those that a mesh axis runs over, the one named last changes fastest.
Arguments:
- mismatch: float32 [8, 128, 32, 128], P('seg', 'slab'), may hold values from -60 to 60, as said below
- advect: float32 [8, 128, 32, 128], P('seg', 'slab'), may hold values from 0.1 to 0.7
- damping: float32 [8, 128, 32, 128], P('seg', 'slab'), may hold values from 0 to 0.2
- axial_shift: int32 [1], replicated, may hold values from 1 to 31
- radius: float32 [1], replicated, may hold values from 0.5 to 2
Outputs:
- step: float32 [8, 128, 32, 128], P('seg', 'slab')
- hessenberg: float32 [3, 2], replicated
Inputs may be any that keep to these rules, and one draw needn't show every extreme that they name: mismatch is finite and of order one to ten.
All inputs are finite; a program needn't handle non-finite values.
Results may differ from a plain program's by a relative error of at most 0.00012.
Values sent between devices are 32-bit elements; how exact they have to be, the bound alone decides.
A program may use at most 64 MiB of HBM per device.

v0:
```python
import jax
import jax.numpy as jnp
from jax import lax
from jax.sharding import PartitionSpec as P

STEPS = 8
KRY = 2


KAPPA = 0.15


def with_halo(cells, sides, width):
    for axis, dim in sides:
        count = lax.axis_size(axis)
        head = lax.slice_in_dim(cells, 0, width, axis=dim)
        tail = lax.slice_in_dim(cells, cells.shape[dim] - width, cells.shape[dim], axis=dim)
        cells = jnp.concatenate(
            [
                lax.ppermute(tail, axis, [(i, (i + 1) % count) for i in range(count)]),
                cells,
                lax.ppermute(head, axis, [((i + 1) % count, i) for i in range(count)]),
            ],
            axis=dim,
        )
    return cells


def from_behind(value, axis, steps):
    count = lax.axis_size(axis)
    pairs = [(source, (source + steps) % count) for source in range(count)]
    return lax.ppermute(value, axis, pairs)


def advance(centre, z_ahead, z_behind, advect, damping):
    wall_zero = jnp.zeros_like(centre[..., :1, :])
    r_outer = jnp.concatenate([centre[..., 1:, :], wall_zero], axis=-2)
    r_inner = jnp.concatenate([wall_zero, centre[..., :-1, :]], axis=-2)
    t_ahead = jnp.roll(centre, -1, axis=-1)
    t_behind = jnp.roll(centre, 1, axis=-1)
    return (
        centre
        + KAPPA * (z_ahead + z_behind + r_outer + r_inner + t_ahead + t_behind - 6.0 * centre)
        - 0.5 * advect * (z_ahead - z_behind)
        - damping * centre
    )


def hookstep(hessenberg, rhs_norm, radius):
    normal = jnp.dot(hessenberg.T, hessenberg, precision=lax.Precision.HIGHEST)
    normal = normal + jnp.eye(KRY, dtype=jnp.float32) / (radius[0] * radius[0])
    target = rhs_norm * hessenberg[0]
    factor = jnp.linalg.cholesky(normal)
    forward = []
    for pivot in range(KRY):
        running = target[pivot]
        for across in range(pivot):
            running = running - factor[pivot, across] * forward[across]
        forward.append(running / factor[pivot, pivot])
    result = [None] * KRY
    for pivot in reversed(range(KRY)):
        running = forward[pivot]
        for across in range(pivot + 1, KRY):
            running = running - factor[across, pivot] * result[across]
        result[pivot] = running / factor[pivot, pivot]
    return result


def quad_form(left, gram_matrix, right):
    return jnp.dot(
        left,
        jnp.dot(gram_matrix, right, precision=lax.Precision.HIGHEST),
        precision=lax.Precision.HIGHEST,
    )


def local(mismatch, advect, damping, axial_shift, radius):
    slab_len = mismatch.shape[1]
    seg_place = lax.axis_index("seg")
    seg_total = lax.axis_size("seg")
    rhs_total = lax.psum(jnp.sum(mismatch * mismatch), ("seg", "slab"))
    rhs_norm = jnp.sqrt(rhs_total)
    powers = [mismatch]
    for column in range(KRY):
        direction = powers[-1]
        current = direction
        for repeat in range(STEPS):
            padded = with_halo(current, (("slab", 1),), 1)
            current = advance(padded[:, 1:-1], padded[:, 2:], padded[:, :-2], advect, damping)
        following = from_behind(direction, "seg", -1)
        jacobian_previous = from_behind(following, "slab", 1)
        joined = jnp.concatenate([jacobian_previous, following], axis=1)
        start = slab_len - axial_shift[0]
        coupled = jnp.where(
            seg_place == seg_total - 1,
            lax.dynamic_slice_in_dim(joined, start, slab_len, axis=1),
            following,
        )
        powers.append(current - coupled)
    count = KRY + 1
    pair_list = []
    local_pairs = []
    for row in range(count):
        for col in range(row, count):
            pair_list.append((row, col))
            local_pairs.append(jnp.sum(powers[row] * powers[col]))
    totals = lax.psum(jnp.stack(local_pairs), ("seg", "slab"))
    gram_rows = [[None] * count for row in range(count)]
    for place, (row, col) in enumerate(pair_list):
        gram_rows[row][col] = totals[place]
        gram_rows[col][row] = totals[place]
    gram_matrix = jnp.stack([jnp.stack(entries) for entries in gram_rows])
    basis = [jnp.zeros((count,), jnp.float32).at[0].set(1.0) / rhs_norm]
    columns = []
    for column in range(KRY):
        image = jnp.concatenate([jnp.zeros((1,), jnp.float32), basis[column][:-1]])
        projected = jnp.stack([quad_form(vector, gram_matrix, image) for vector in basis])
        for member in range(column + 1):
            image = image - projected[member] * basis[member]
        new_norm = jnp.sqrt(quad_form(image, gram_matrix, image))
        columns.append(
            jnp.concatenate(
                [projected, new_norm[None], jnp.zeros((KRY - column - 1,), jnp.float32)]
            )
        )
        basis.append(image / new_norm)
    hessenberg = jnp.stack(columns, axis=1)
    weights = hookstep(hessenberg, rhs_norm, radius)
    mixing = weights[0] * basis[0]
    member = 1
    mixing = mixing + weights[member] * basis[member]
    step = mixing[0] * powers[0]
    for member in range(1, count):
        step = step + mixing[member] * powers[member]
    return (step, hessenberg)


def solution(mesh):
    in_specs = (
        P("seg", "slab", None, None),
        P("seg", "slab", None, None),
        P("seg", "slab", None, None),
        P(),
        P(),
    )
    out_specs = (P("seg", "slab", None, None), P())
    return jax.shard_map(local, mesh=mesh, in_specs=in_specs, out_specs=out_specs, check_vma=False)
```

profile of v0, /device:TPU:0, one launch (start us, length us, event | category | flops | bytes accessed | tf_op | source)
XLA Modules:
  0.0 200.0 jit_solution(3831343964644363961)
XLA Ops:
  0.6 3.4 %collective-permute-start.16 = (f32[1,32,32,128]{3,2,1,0:T(8,128)}, f32[1,32,32,128]{3,2,1,0:T(8,128)}, u32[]{:S(2)}, u32[]{:S(2)}) collective-permute-start(f32[1,32,32,128]{3,2,1,0:T(8,128)} %param.7), channel_id=1, source_target_pairs={{0,28},{4,0},{8,4},{12,8},{16,12},{20,16},{24,20},{28,24},{1,29},{... | collective-permute-start | bytes 1572872 | tf_op jit(solution)/shard_map/ppermute | solution.py:32
  4.8 3.6 %collective-permute-start = (f32[1,1,32,128]{3,2,1,0:T(8,128)S(1)}, f32[1,1,32,128]{3,2,1,0:T(8,128)S(1)}, u32[]{:S(2)}, u32[]{:S(2)}) collective-permute-start(f32[1,1,32,128]{3,2,1,0:T(8,128)S(1)} %get-tuple-element.146), channel_id=1, source_target_pairs={{1,0},{2,1},{3,2},{0,3},{5,4},{6,5},{7,6},{4,7},{9,8},{10,9},{11,1... | collective-permute-start | bytes 49160 | tf_op jit(solution)/shard_map/ppermute | solution.py:22
  16.2 3.2 %collective-permute-start.2 = (f32[1,1,32,128]{3,2,1,0:T(8,128)S(1)}, f32[1,1,32,128]{3,2,1,0:T(8,128)S(1)}, u32[]{:S(2)}, u32[]{:S(2)}) collective-permute-start(f32[1,1,32,128]{3,2,1,0:T(8,128)S(1)} %get-tuple-element.138), channel_id=1, source_target_pairs={{1,0},{2,1},{3,2},{0,3},{5,4},{6,5},{7,6},{4,7},{9,8},{10,9},{11,1... | collective-permute-start | bytes 49160 | tf_op jit(solution)/shard_map/ppermute | solution.py:22
  20.9 4.1 %collective-permute-done.3 = f32[1,1,32,128]{3,2,1,0:T(8,128)S(1)} collective-permute-done((f32[1,1,32,128]{3,2,1,0:T(8,128)S(1)}, f32[1,1,32,128]{3,2,1,0:T(8,128)S(1)}, u32[]{:S(2)}, u32[]{:S(2)}) %collective-permute-start.3) | collective-permute-done | bytes 16416 | tf_op jit(solution)/shard_map/ppermute | solution.py:20
  26.0 2.0 %collective-permute-start.5 = (f32[1,1,32,128]{3,2,1,0:T(8,128)S(1)}, f32[1,1,32,128]{3,2,1,0:T(8,128)S(1)}, u32[]{:S(2)}, u32[]{:S(2)}) collective-permute-start(f32[1,1,32,128]{3,2,1,0:T(8,128)S(1)} %get-tuple-element.129), channel_id=1, source_target_pairs={{0,1},{1,2},{2,3},{3,0},{4,5},{5,6},{6,7},{7,4},{8,9},{9,10},{10,1... | collective-permute-start | bytes 49160 | tf_op jit(solution)/shard_map/ppermute | solution.py:20
  32.5 2.0 %collective-permute-start.7 = (f32[1,1,32,128]{3,2,1,0:T(8,128)S(1)}, f32[1,1,32,128]{3,2,1,0:T(8,128)S(1)}, u32[]{:S(2)}, u32[]{:S(2)}) collective-permute-start(f32[1,1,32,128]{3,2,1,0:T(8,128)S(1)} %get-tuple-element.121), channel_id=1, source_target_pairs={{0,1},{1,2},{2,3},{3,0},{4,5},{5,6},{6,7},{7,4},{8,9},{9,10},{10,1... | collective-permute-start | bytes 49160 | tf_op jit(solution)/shard_map/ppermute | solution.py:20
  39.3 2.0 %collective-permute-start.9 = (f32[1,1,32,128]{3,2,1,0:T(8,128)S(1)}, f32[1,1,32,128]{3,2,1,0:T(8,128)S(1)}, u32[]{:S(2)}, u32[]{:S(2)}) collective-permute-start(f32[1,1,32,128]{3,2,1,0:T(8,128)S(1)} %get-tuple-element.113), channel_id=1, source_target_pairs={{0,1},{1,2},{2,3},{3,0},{4,5},{5,6},{6,7},{7,4},{8,9},{9,10},{10,1... | collective-permute-start | bytes 49160 | tf_op jit(solution)/shard_map/ppermute | solution.py:20
  45.9 2.0 %collective-permute-start.11 = (f32[1,1,32,128]{3,2,1,0:T(8,128)S(1)}, f32[1,1,32,128]{3,2,1,0:T(8,128)S(1)}, u32[]{:S(2)}, u32[]{:S(2)}) collective-permute-start(f32[1,1,32,128]{3,2,1,0:T(8,128)S(1)} %get-tuple-element.105), channel_id=1, source_target_pairs={{0,1},{1,2},{2,3},{3,0},{4,5},{5,6},{6,7},{7,4},{8,9},{9,10},{10,1... | collective-permute-start | bytes 49160 | tf_op jit(solution)/shard_map/ppermute | solution.py:20
  52.5 2.0 %collective-permute-start.13 = (f32[1,1,32,128]{3,2,1,0:T(8,128)S(1)}, f32[1,1,32,128]{3,2,1,0:T(8,128)S(1)}, u32[]{:S(2)}, u32[]{:S(2)}) collective-permute-start(f32[1,1,32,128]{3,2,1,0:T(8,128)S(1)} %get-tuple-element.97), channel_id=1, source_target_pairs={{0,1},{1,2},{2,3},{3,0},{4,5},{5,6},{6,7},{7,4},{8,9},{9,10},{10,1... | collective-permute-start | bytes 49160 | tf_op jit(solution)/shard_map/ppermute | solution.py:20
  56.2 2.1 %collective-permute-done.13 = f32[1,1,32,128]{3,2,1,0:T(8,128)S(1)} collective-permute-done((f32[1,1,32,128]{3,2,1,0:T(8,128)S(1)}, f32[1,1,32,128]{3,2,1,0:T(8,128)S(1)}, u32[]{:S(2)}, u32[]{:S(2)}) %collective-permute-start.13) | collective-permute-done | bytes 16416 | tf_op jit(solution)/shard_map/ppermute | solution.py:20
  59.0 2.0 %collective-permute-start.15 = (f32[1,1,32,128]{3,2,1,0:T(8,128)S(1)}, f32[1,1,32,128]{3,2,1,0:T(8,128)S(1)}, u32[]{:S(2)}, u32[]{:S(2)}) collective-permute-start(f32[1,1,32,128]{3,2,1,0:T(8,128)S(1)} %get-tuple-element.89), channel_id=1, source_target_pairs={{0,1},{1,2},{2,3},{3,0},{4,5},{5,6},{6,7},{7,4},{8,9},{9,10},{10,1... | collective-permute-start | bytes 49160 | tf_op jit(solution)/shard_map/ppermute | solution.py:20
  64.6 8.1 %collective-permute-done.17 = f32[1,32,32,128]{3,2,1,0:T(8,128)S(1)} collective-permute-done((f32[1,32,32,128]{3,2,1,0:T(8,128)}, f32[1,32,32,128]{3,2,1,0:T(8,128)S(1)}, u32[]{:S(2)}, u32[]{:S(2)}) %collective-permute-start.17) | collective-permute-done | bytes 524320 | tf_op jit(solution)/shard_map/ppermute | solution.py:32
  81.6 2.0 %collective-permute-start.21 = (f32[1,1,32,128]{3,2,1,0:T(8,128)S(1)}, f32[1,1,32,128]{3,2,1,0:T(8,128)S(1)}, u32[]{:S(2)}, u32[]{:S(2)}) collective-permute-start(f32[1,1,32,128]{3,2,1,0:T(8,128)S(1)} %get-tuple-element.73), channel_id=1, source_target_pairs={{0,1},{1,2},{2,3},{3,0},{4,5},{5,6},{6,7},{7,4},{8,9},{9,10},{10,1... | collective-permute-start | bytes 49160 | tf_op jit(solution)/shard_map/ppermute | solution.py:20
  85.3 2.0 %collective-permute-done.21 = f32[1,1,32,128]{3,2,1,0:T(8,128)S(1)} collective-permute-done((f32[1,1,32,128]{3,2,1,0:T(8,128)S(1)}, f32[1,1,32,128]{3,2,1,0:T(8,128)S(1)}, u32[]{:S(2)}, u32[]{:S(2)}) %collective-permute-start.21) | collective-permute-done | bytes 16416 | tf_op jit(solution)/shard_map/ppermute | solution.py:20
  88.4 2.0 %collective-permute-start.23 = (f32[1,1,32,128]{3,2,1,0:T(8,128)S(1)}, f32[1,1,32,128]{3,2,1,0:T(8,128)S(1)}, u32[]{:S(2)}, u32[]{:S(2)}) collective-permute-start(f32[1,1,32,128]{3,2,1,0:T(8,128)S(1)} %get-tuple-element.65), channel_id=1, source_target_pairs={{0,1},{1,2},{2,3},{3,0},{4,5},{5,6},{6,7},{7,4},{8,9},{9,10},{10,1... | collective-permute-start | bytes 49160 | tf_op jit(solution)/shard_map/ppermute | solution.py:20
  95.0 2.0 %collective-permute-start.25 = (f32[1,1,32,128]{3,2,1,0:T(8,128)S(1)}, f32[1,1,32,128]{3,2,1,0:T(8,128)S(1)}, u32[]{:S(2)}, u32[]{:S(2)}) collective-permute-start(f32[1,1,32,128]{3,2,1,0:T(8,128)S(1)} %get-tuple-element.57), channel_id=1, source_target_pairs={{0,1},{1,2},{2,3},{3,0},{4,5},{5,6},{6,7},{7,4},{8,9},{9,10},{10,1... | collective-permute-start | bytes 49160 | tf_op jit(solution)/shard_map/ppermute | solution.py:20
  101.6 2.0 %collective-permute-start.27 = (f32[1,1,32,128]{3,2,1,0:T(8,128)S(1)}, f32[1,1,32,128]{3,2,1,0:T(8,128)S(1)}, u32[]{:S(2)}, u32[]{:S(2)}) collective-permute-start(f32[1,1,32,128]{3,2,1,0:T(8,128)S(1)} %get-tuple-element.49), channel_id=1, source_target_pairs={{0,1},{1,2},{2,3},{3,0},{4,5},{5,6},{6,7},{7,4},{8,9},{9,10},{10,1... | collective-permute-start | bytes 49160 | tf_op jit(solution)/shard_map/ppermute | solution.py:20
  114.8 2.0 %collective-permute-start.31 = (f32[1,1,32,128]{3,2,1,0:T(8,128)S(1)}, f32[1,1,32,128]{3,2,1,0:T(8,128)S(1)}, u32[]{:S(2)}, u32[]{:S(2)}) collective-permute-start(f32[1,1,32,128]{3,2,1,0:T(8,128)S(1)} %get-tuple-element.33), channel_id=1, source_target_pairs={{0,1},{1,2},{2,3},{3,0},{4,5},{5,6},{6,7},{7,4},{8,9},{9,10},{10,1... | collective-permute-start | bytes 49160 | tf_op jit(solution)/shard_map/ppermute | solution.py:20
  118.5 2.0 %collective-permute-done.31 = f32[1,1,32,128]{3,2,1,0:T(8,128)S(1)} collective-permute-done((f32[1,1,32,128]{3,2,1,0:T(8,128)S(1)}, f32[1,1,32,128]{3,2,1,0:T(8,128)S(1)}, u32[]{:S(2)}, u32[]{:S(2)}) %collective-permute-start.31) | collective-permute-done | bytes 16416 | tf_op jit(solution)/shard_map/ppermute | solution.py:20
  126.8 7.6 %collective-permute-done.35 = f32[1,32,32,128]{3,2,1,0:T(8,128)S(1)} collective-permute-done((f32[1,32,32,128]{3,2,1,0:T(8,128)S(1)}, f32[1,32,32,128]{3,2,1,0:T(8,128)S(1)}, u32[]{:S(2)}, u32[]{:S(2)}) %collective-permute-start.35) | collective-permute-done | bytes 524320 | tf_op jit(solution)/shard_map/ppermute | solution.py:32
  135.9 3.8 %stack.67 = f32[6]{0:T(128)S(1)} concatenate(f32[1]{0:T(128)} %bitcast, f32[1]{0:T(128)} %bitcast.3, f32[1]{0:T(128)} %bitcast.4, f32[1]{0:T(128)} %bitcast.5, f32[1]{0:T(128)} %bitcast.6, f32[1]{0:T(128)} %bitcast.7), dimensions={0} | concatenate | bytes 48 | tf_op jit(solution)/shard_map/stack | solution.py:107
  139.8 37.1 %all-reduce.32 = (f32[]{:T(128)}, f32[6]{0:T(128)S(1)}) all-reduce(f32[]{:T(128)} %get-tuple-element.19, f32[6]{0:T(128)S(1)} %stack.67), channel_id=1, replica_groups=mesh['seg'=8,'slab'=4] {'seg','slab'}, use_global_device_ids=true, to_apply=%region_1.0 | all-reduce | flops 7 | bytes 56 | tf_op jit(solution)/shard_map/psum | solution.py:81
  183.4 2.0 %fusion.3 = f32[]{:T(128)} fusion(f32[3]{0:T(128)S(1)} %broadcast_divide_fusion, f32[3]{0:T(128)S(1)} %broadcast_divide_fusion.1, f32[]{:T(128)} %get-tuple-element.21, f32[]{:T(128)} %get-tuple-element.20, f32[2]{0:T(128)S(1)} %bitcast.75, f32[1]{0:T(128)} %constant.93.clone.1, f32[1,3]{1,0:T(1,128)S(1)} %get-tuple-element.166, ...), kind=kOutput, calls=%fused_computation.11 | convolution fusion | flops 161 | bytes 84 | tf_op jit(solution)/shard_map/dot_general | solution.py:72
  197.2 2.8 %multiply_add_fusion = f32[1,32,32,128]{3,2,1,0:T(8,128)} fusion(f32[1,32,32,128]{3,2,1,0:T(8,128)S(1)} %get-tuple-element.24, f32[1,32,32,128]{3,2,1,0:T(8,128)S(1)} %fusion.11, f32[1,32,32,128]{3,2,1,0:T(8,128)S(1)} %copy-done.2, f32[]{:T(128)} %bitcast.35, f32[]{:T(128)} %bitcast.34, f32[]{:T(128)} %bitcast.33), kind=kLoop, calls=%fused_computation.164 | loop fusion | flops 655360 | bytes 2097164 | tf_op jit(solution)/shard_map/add | solution.py:134
  (167 shorter events, 86.4 us)
Async XLA Ops:
  0.6 60.5 %collective-permute-start.16 = (f32[1,32,32,128]{3,2,1,0:T(8,128)}, f32[1,32,32,128]{3,2,1,0:T(8,128)}, u32[]{:S(2)}, u32[]{:S(2)}) collective-permute-start(f32[1,32,32,128]{3,2,1,0:T(8,128)} %param.7), channel_id=1, source_target_pairs={{0,28},{4,0},{8,4},{12,8},{16,12},{20,16},{24,20},{28,24},{1,29},{... | collective-permute-start | bytes 1572872 | tf_op jit(solution)/shard_map/ppermute | solution.py:32
  4.8 8.5 %collective-permute-start = (f32[1,1,32,128]{3,2,1,0:T(8,128)S(1)}, f32[1,1,32,128]{3,2,1,0:T(8,128)S(1)}, u32[]{:S(2)}, u32[]{:S(2)}) collective-permute-start(f32[1,1,32,128]{3,2,1,0:T(8,128)S(1)} %get-tuple-element.146), channel_id=1, source_target_pairs={{1,0},{2,1},{3,2},{0,3},{5,4},{6,5},{7,6},{4,7},{9,8},{10,9},{11,1... | collective-permute-start | bytes 49160 | tf_op jit(solution)/shard_map/ppermute | solution.py:22
  8.4 5.5 %collective-permute-start.1 = (f32[1,1,32,128]{3,2,1,0:T(8,128)S(1)}, f32[1,1,32,128]{3,2,1,0:T(8,128)S(1)}, u32[]{:S(2)}, u32[]{:S(2)}) collective-permute-start(f32[1,1,32,128]{3,2,1,0:T(8,128)S(1)} %get-tuple-element.145), channel_id=1, source_target_pairs={{0,1},{1,2},{2,3},{3,0},{4,5},{5,6},{6,7},{7,4},{8,9},{9,10},{10,1... | collective-permute-start | bytes 49160 | tf_op jit(solution)/shard_map/ppermute | solution.py:20
  16.2 4.7 %collective-permute-start.2 = (f32[1,1,32,128]{3,2,1,0:T(8,128)S(1)}, f32[1,1,32,128]{3,2,1,0:T(8,128)S(1)}, u32[]{:S(2)}, u32[]{:S(2)}) collective-permute-start(f32[1,1,32,128]{3,2,1,0:T(8,128)S(1)} %get-tuple-element.138), channel_id=1, source_target_pairs={{1,0},{2,1},{3,2},{0,3},{5,4},{6,5},{7,6},{4,7},{9,8},{10,9},{11,1... | collective-permute-start | bytes 49160 | tf_op jit(solution)/shard_map/ppermute | solution.py:22
  19.4 5.5 %collective-permute-start.3 = (f32[1,1,32,128]{3,2,1,0:T(8,128)S(1)}, f32[1,1,32,128]{3,2,1,0:T(8,128)S(1)}, u32[]{:S(2)}, u32[]{:S(2)}) collective-permute-start(f32[1,1,32,128]{3,2,1,0:T(8,128)S(1)} %get-tuple-element.137), channel_id=1, source_target_pairs={{0,1},{1,2},{2,3},{3,0},{4,5},{5,6},{6,7},{7,4},{8,9},{9,10},{10,1... | collective-permute-start | bytes 49160 | tf_op jit(solution)/shard_map/ppermute | solution.py:20
  26.0 5.6 %collective-permute-start.5 = (f32[1,1,32,128]{3,2,1,0:T(8,128)S(1)}, f32[1,1,32,128]{3,2,1,0:T(8,128)S(1)}, u32[]{:S(2)}, u32[]{:S(2)}) collective-permute-start(f32[1,1,32,128]{3,2,1,0:T(8,128)S(1)} %get-tuple-element.129), channel_id=1, source_target_pairs={{0,1},{1,2},{2,3},{3,0},{4,5},{5,6},{6,7},{7,4},{8,9},{9,10},{10,1... | collective-permute-start | bytes 49160 | tf_op jit(solution)/shard_map/ppermute | solution.py:20
  32.5 3.9 %collective-permute-start.6 = (f32[1,1,32,128]{3,2,1,0:T(8,128)S(1)}, f32[1,1,32,128]{3,2,1,0:T(8,128)S(1)}, u32[]{:S(2)}, u32[]{:S(2)}) collective-permute-start(f32[1,1,32,128]{3,2,1,0:T(8,128)S(1)} %get-tuple-element.122), channel_id=1, source_target_pairs={{1,0},{2,1},{3,2},{0,3},{5,4},{6,5},{7,6},{4,7},{9,8},{10,9},{11,1... | collective-permute-start | bytes 49160 | tf_op jit(solution)/shard_map/ppermute | solution.py:22
  32.5 5.7 %collective-permute-start.7 = (f32[1,1,32,128]{3,2,1,0:T(8,128)S(1)}, f32[1,1,32,128]{3,2,1,0:T(8,128)S(1)}, u32[]{:S(2)}, u32[]{:S(2)}) collective-permute-start(f32[1,1,32,128]{3,2,1,0:T(8,128)S(1)} %get-tuple-element.121), channel_id=1, source_target_pairs={{0,1},{1,2},{2,3},{3,0},{4,5},{5,6},{6,7},{7,4},{8,9},{9,10},{10,1... | collective-permute-start | bytes 49160 | tf_op jit(solution)/shard_map/ppermute | solution.py:20
  39.3 5.6 %collective-permute-start.9 = (f32[1,1,32,128]{3,2,1,0:T(8,128)S(1)}, f32[1,1,32,128]{3,2,1,0:T(8,128)S(1)}, u32[]{:S(2)}, u32[]{:S(2)}) collective-permute-start(f32[1,1,32,128]{3,2,1,0:T(8,128)S(1)} %get-tuple-element.113), channel_id=1, source_target_pairs={{0,1},{1,2},{2,3},{3,0},{4,5},{5,6},{6,7},{7,4},{8,9},{9,10},{10,1... | collective-permute-start | bytes 49160 | tf_op jit(solution)/shard_map/ppermute | solution.py:20
  45.9 5.6 %collective-permute-start.11 = (f32[1,1,32,128]{3,2,1,0:T(8,128)S(1)}, f32[1,1,32,128]{3,2,1,0:T(8,128)S(1)}, u32[]{:S(2)}, u32[]{:S(2)}) collective-permute-start(f32[1,1,32,128]{3,2,1,0:T(8,128)S(1)} %get-tuple-element.105), channel_id=1, source_target_pairs={{0,1},{1,2},{2,3},{3,0},{4,5},{5,6},{6,7},{7,4},{8,9},{9,10},{10,1... | collective-permute-start | bytes 49160 | tf_op jit(solution)/shard_map/ppermute | solution.py:20
  52.5 5.8 %collective-permute-start.13 = (f32[1,1,32,128]{3,2,1,0:T(8,128)S(1)}, f32[1,1,32,128]{3,2,1,0:T(8,128)S(1)}, u32[]{:S(2)}, u32[]{:S(2)}) collective-permute-start(f32[1,1,32,128]{3,2,1,0:T(8,128)S(1)} %get-tuple-element.97), channel_id=1, source_target_pairs={{0,1},{1,2},{2,3},{3,0},{4,5},{5,6},{6,7},{7,4},{8,9},{9,10},{10,1... | collective-permute-start | bytes 49160 | tf_op jit(solution)/shard_map/ppermute | solution.py:20
  59.0 5.6 %collective-permute-start.15 = (f32[1,1,32,128]{3,2,1,0:T(8,128)S(1)}, f32[1,1,32,128]{3,2,1,0:T(8,128)S(1)}, u32[]{:S(2)}, u32[]{:S(2)}) collective-permute-start(f32[1,1,32,128]{3,2,1,0:T(8,128)S(1)} %get-tuple-element.89), channel_id=1, source_target_pairs={{0,1},{1,2},{2,3},{3,0},{4,5},{5,6},{6,7},{7,4},{8,9},{9,10},{10,1... | collective-permute-start | bytes 49160 | tf_op jit(solution)/shard_map/ppermute | solution.py:20
  61.1 11.5 %collective-permute-start.17 = (f32[1,32,32,128]{3,2,1,0:T(8,128)}, f32[1,32,32,128]{3,2,1,0:T(8,128)S(1)}, u32[]{:S(2)}, u32[]{:S(2)}) collective-permute-start(f32[1,32,32,128]{3,2,1,0:T(8,128)} %collective-permute-done.16), channel_id=1, source_target_pairs={{0,1},{1,2},{2,3},{3,0},{4,5},{5,6},{6,7},{7,4},{8,9},{9,10},{10,1... | collective-permute-start | bytes 1572872 | tf_op jit(solution)/shard_map/ppermute | solution.py:32
  75.0 5.5 %collective-permute-start.19 = (f32[1,1,32,128]{3,2,1,0:T(8,128)S(1)}, f32[1,1,32,128]{3,2,1,0:T(8,128)S(1)}, u32[]{:S(2)}, u32[]{:S(2)}) collective-permute-start(f32[1,1,32,128]{3,2,1,0:T(8,128)S(1)} %get-tuple-element.81), channel_id=1, source_target_pairs={{0,1},{1,2},{2,3},{3,0},{4,5},{5,6},{6,7},{7,4},{8,9},{9,10},{10,1... | collective-permute-start | bytes 49160 | tf_op jit(solution)/shard_map/ppermute | solution.py:20
  77.1 46.2 %collective-permute-start.34 = (f32[1,32,32,128]{3,2,1,0:T(8,128)S(1)}, f32[1,32,32,128]{3,2,1,0:T(8,128)S(1)}, u32[]{:S(2)}, u32[]{:S(2)}) collective-permute-start(f32[1,32,32,128]{3,2,1,0:T(8,128)S(1)} %fusion.11), channel_id=1, source_target_pairs={{0,28},{4,0},{8,4},{12,8},{16,12},{20,16},{24,20},{28,24},{1,29},{... | collective-permute-start | bytes 1572872 | tf_op jit(solution)/shard_map/ppermute | solution.py:32
  81.6 5.8 %collective-permute-start.21 = (f32[1,1,32,128]{3,2,1,0:T(8,128)S(1)}, f32[1,1,32,128]{3,2,1,0:T(8,128)S(1)}, u32[]{:S(2)}, u32[]{:S(2)}) collective-permute-start(f32[1,1,32,128]{3,2,1,0:T(8,128)S(1)} %get-tuple-element.73), channel_id=1, source_target_pairs={{0,1},{1,2},{2,3},{3,0},{4,5},{5,6},{6,7},{7,4},{8,9},{9,10},{10,1... | collective-permute-start | bytes 49160 | tf_op jit(solution)/shard_map/ppermute | solution.py:20
  88.4 5.6 %collective-permute-start.23 = (f32[1,1,32,128]{3,2,1,0:T(8,128)S(1)}, f32[1,1,32,128]{3,2,1,0:T(8,128)S(1)}, u32[]{:S(2)}, u32[]{:S(2)}) collective-permute-start(f32[1,1,32,128]{3,2,1,0:T(8,128)S(1)} %get-tuple-element.65), channel_id=1, source_target_pairs={{0,1},{1,2},{2,3},{3,0},{4,5},{5,6},{6,7},{7,4},{8,9},{9,10},{10,1... | collective-permute-start | bytes 49160 | tf_op jit(solution)/shard_map/ppermute | solution.py:20
  95.0 5.6 %collective-permute-start.25 = (f32[1,1,32,128]{3,2,1,0:T(8,128)S(1)}, f32[1,1,32,128]{3,2,1,0:T(8,128)S(1)}, u32[]{:S(2)}, u32[]{:S(2)}) collective-permute-start(f32[1,1,32,128]{3,2,1,0:T(8,128)S(1)} %get-tuple-element.57), channel_id=1, source_target_pairs={{0,1},{1,2},{2,3},{3,0},{4,5},{5,6},{6,7},{7,4},{8,9},{9,10},{10,1... | collective-permute-start | bytes 49160 | tf_op jit(solution)/shard_map/ppermute | solution.py:20
  101.6 5.6 %collective-permute-start.27 = (f32[1,1,32,128]{3,2,1,0:T(8,128)S(1)}, f32[1,1,32,128]{3,2,1,0:T(8,128)S(1)}, u32[]{:S(2)}, u32[]{:S(2)}) collective-permute-start(f32[1,1,32,128]{3,2,1,0:T(8,128)S(1)} %get-tuple-element.49), channel_id=1, source_target_pairs={{0,1},{1,2},{2,3},{3,0},{4,5},{5,6},{6,7},{7,4},{8,9},{9,10},{10,1... | collective-permute-start | bytes 49160 | tf_op jit(solution)/shard_map/ppermute | solution.py:20
  108.2 5.6 %collective-permute-start.29 = (f32[1,1,32,128]{3,2,1,0:T(8,128)S(1)}, f32[1,1,32,128]{3,2,1,0:T(8,128)S(1)}, u32[]{:S(2)}, u32[]{:S(2)}) collective-permute-start(f32[1,1,32,128]{3,2,1,0:T(8,128)S(1)} %get-tuple-element.41), channel_id=1, source_target_pairs={{0,1},{1,2},{2,3},{3,0},{4,5},{5,6},{6,7},{7,4},{8,9},{9,10},{10,1... | collective-permute-start | bytes 49160 | tf_op jit(solution)/shard_map/ppermute | solution.py:20
  114.8 5.8 %collective-permute-start.31 = (f32[1,1,32,128]{3,2,1,0:T(8,128)S(1)}, f32[1,1,32,128]{3,2,1,0:T(8,128)S(1)}, u32[]{:S(2)}, u32[]{:S(2)}) collective-permute-start(f32[1,1,32,128]{3,2,1,0:T(8,128)S(1)} %get-tuple-element.33), channel_id=1, source_target_pairs={{0,1},{1,2},{2,3},{3,0},{4,5},{5,6},{6,7},{7,4},{8,9},{9,10},{10,1... | collective-permute-start | bytes 49160 | tf_op jit(solution)/shard_map/ppermute | solution.py:20
  121.1 4.1 %collective-permute-start.32 = (f32[1,1,32,128]{3,2,1,0:T(8,128)S(1)}, f32[1,1,32,128]{3,2,1,0:T(8,128)S(1)}, u32[]{:S(2)}, u32[]{:S(2)}) collective-permute-start(f32[1,1,32,128]{3,2,1,0:T(8,128)S(1)} %get-tuple-element.25), channel_id=1, source_target_pairs={{1,0},{2,1},{3,2},{0,3},{5,4},{6,5},{7,6},{4,7},{9,8},{10,9},{11,1... | collective-permute-start | bytes 49160 | tf_op jit(solution)/shard_map/ppermute | solution.py:22
  121.2 5.6 %collective-permute-start.33 = (f32[1,1,32,128]{3,2,1,0:T(8,128)S(1)}, f32[1,1,32,128]{3,2,1,0:T(8,128)S(1)}, u32[]{:S(2)}, u32[]{:S(2)}) collective-permute-start(f32[1,1,32,128]{3,2,1,0:T(8,128)S(1)} %get-tuple-element.26), channel_id=1, source_target_pairs={{0,1},{1,2},{2,3},{3,0},{4,5},{5,6},{6,7},{7,4},{8,9},{9,10},{10,1... | collective-permute-start | bytes 49160 | tf_op jit(solution)/shard_map/ppermute | solution.py:20
  123.3 11.0 %collective-permute-start.35 = (f32[1,32,32,128]{3,2,1,0:T(8,128)S(1)}, f32[1,32,32,128]{3,2,1,0:T(8,128)S(1)}, u32[]{:S(2)}, u32[]{:S(2)}) collective-permute-start(f32[1,32,32,128]{3,2,1,0:T(8,128)S(1)} %collective-permute-done.34), channel_id=1, source_target_pairs={{0,1},{1,2},{2,3},{3,0},{4,5},{5,6},{6,7},{7,4},{8,9},{9,10},{10,1... | collective-permute-start | bytes 1572872 | tf_op jit(solution)/shard_map/ppermute | solution.py:32
  (17 other events, 54.5 us)
where the time goes:
time: 202 us; the launch traced here: 200 us
  waiting for transfers between devices  68.5 us (34%)
  starting transfers between devices  39.7 us (20%)
  blocking collectives  37.1 us (18%)
  other arithmetic  21.7 us (11%)
  local copies, waits for them, and re-layouts  18.9 us (9%)
  between operations  9.64 us (5%)
  matrix products  4.53 us (2%)
    psum x1, blocking collectives, local(): rhs_total = lax.psum(jnp.sum(mismatch * mismatch), ('seg', 'slab'))  37.1 us
    ppermute x16, waiting for transfers between devices, with_halo(): lax.ppermute(tail, axis, [(i, (i + 1) % count) for i in range(count)])  31.2 us
    ppermute x16, starting transfers between devices, with_halo(): lax.ppermute(tail, axis, [(i, (i + 1) % count) for i in range(count)])  28 us
    ppermute x16, waiting for transfers between devices, with_halo(): lax.ppermute(head, axis, [((i + 1) % count, i) for i in range(count)])  21.6 us
    ppermute x4, waiting for transfers between devices, from_behind(): return lax.ppermute(value, axis, pairs)  15.6 us
    sub x14, other arithmetic, advance(): centre + KAPPA * (z_ahead + z_behind + r_outer + r_inner + t_ahead + t_be...  9.84 us
    slice x30, local copies, waits for them, and re-layouts, advance(): t_behind = jnp.roll(centre, 1, axis=-1)  7.89 us
    ppermute x16, starting transfers between devices, with_halo(): lax.ppermute(head, axis, [((i + 1) % count, i) for i in range(count)])  7.81 us
  transfers between devices with their start and end apart: 36, of which 33 were waited for; matrix products, arithmetic and copies ran while one was open for 11% of the time, Pallas kernels for 0%

commit v1 on v0

v1 whole, which is shorter than its diff:
```python
import functools

import jax
import jax.numpy as jnp
from jax import lax
from jax.experimental import pallas as pl
from jax.experimental.pallas import tpu as pltpu
from jax.sharding import PartitionSpec as P

STEPS = 8
KRY = 2
KAPPA = 0.15
WIDTH = 8

MESH = pl.DeviceIdType.MESH


def stencil(behind, centre, ahead, advect, damping):
    blocks, rows, lanes = centre.shape
    row = lax.broadcasted_iota(jnp.int32, centre.shape, 1)
    wall = jnp.zeros((1, rows, lanes), jnp.float32)
    around = pltpu.roll(centre, 1, 2) + pltpu.roll(centre, lanes - 1, 2)
    down = pltpu.roll(centre, 1, 1)
    up = pltpu.roll(centre, rows - 1, 1)
    inner = jnp.where(row == 0, jnp.concatenate([wall, down[:-1]], axis=0), down)
    outer = jnp.where(row == rows - 1, jnp.concatenate([up[1:], wall], axis=0), up)
    total = (around + (inner + outer)) + (ahead + behind)
    return centre * ((1.0 - 6.0 * KAPPA) - damping) + KAPPA * total + (0.5 * advect) * (behind - ahead)


def krylov_kernel(
    seg_n, slab_n, width,
    shift_ref, p_ref, a_ref, g_ref,
    p1_ref, totals_ref,
    levels, adv, dam, next_a, next_b, seg_sums, slab_sums,
    load_sem, halo_send, halo_recv, pair_send, pair_recv, cross_send, cross_recv,
    out_sem, seg_send, seg_recv, slab_send, slab_recv,
):
    loc = p_ref.shape[0]
    full = loc + 2 * width
    seg = lax.axis_index("seg")
    slab = lax.axis_index("slab")
    at = lambda s, z: {"seg": lax.rem(seg + s, seg_n), "slab": lax.rem(slab + z, slab_n)}
    coupled = (next_a, next_b)

    barrier = pltpu.get_barrier_semaphore()
    peers = [(0, z) for z in range(1, slab_n)] + [(s, 0) for s in range(1, seg_n)]
    peers += [(seg_n - 1, 1), (1, slab_n - 1)]
    for s, z in peers:
        pl.semaphore_signal(barrier, inc=1, device_id=at(s, z), device_id_type=MESH)
    own = pl.ds(width, loc)
    loads = [
        pltpu.make_async_copy(p_ref, levels.at[0, own], load_sem.at[0]),
        pltpu.make_async_copy(a_ref, adv.at[own], load_sem.at[1]),
        pltpu.make_async_copy(g_ref, dam.at[own], load_sem.at[2]),
    ]
    for load in loads:
        load.start()

    def halo(source, first, target, count, place):
        return [
            pltpu.make_async_remote_copy(
                src_ref=source.at[pl.ds(first + loc - count, count)],
                dst_ref=target.at[pl.ds(width - count, count)],
                send_sem=halo_send.at[place, 0], recv_sem=halo_recv.at[place, 0],
                device_id=at(0, 1), device_id_type=MESH,
            ),
            pltpu.make_async_remote_copy(
                src_ref=source.at[pl.ds(first, count)],
                dst_ref=target.at[pl.ds(width + loc, count)],
                send_sem=halo_send.at[place, 1], recv_sem=halo_recv.at[place, 1],
                device_id=at(0, slab_n - 1), device_id_type=MESH,
            ),
        ]

    def pair(source, column):
        return pltpu.make_async_remote_copy(
            src_ref=source, dst_ref=coupled[column].at[pl.ds(loc, loc)],
            send_sem=pair_send.at[column], recv_sem=pair_recv.at[column],
            device_id=at(seg_n - 1, 0), device_id_type=MESH,
        )

    def cross(source, column):
        return pltpu.make_async_remote_copy(
            src_ref=source, dst_ref=coupled[column].at[pl.ds(0, loc)],
            send_sem=cross_send.at[column], recv_sem=cross_recv.at[column],
            device_id=at(seg_n - 1, 1), device_id_type=MESH,
        )

    def sweep(level, start, count):
        before = levels[level, start - 1]
        here = levels[level, start]
        for plane in range(count):
            after = levels[level, start + plane + 1]
            levels[level + 1, start + plane] = stencil(
                before, here, after, adv[start + plane], dam[start + plane]
            )
            before, here = here, after

    thirds = -(-(loc - 2) // 3)

    def interior(base):
        def one(k, carry):
            def piece(i, inner):
                sweep(base + k, width + k + 1 + (i * (loc - 2 - 2 * k - thirds)) // 2, thirds)
                return inner
            return lax.fori_loop(0, 3, piece, carry)
        lax.fori_loop(0, width, one, 0)

    def edges(base):
        def one(k, carry):
            sweep(base + k, k + 1, width)
            sweep(base + k, full - 1 - k - width, width)
            return carry
        lax.fori_loop(0, width, one, 0)

    pl.semaphore_wait(barrier, len(peers))
    exchanges = KRY * STEPS // width
    sent = halo(p_ref, 0, levels.at[0], width, 0)
    sent += halo(a_ref, 0, adv, width - 1, exchanges)
    sent += halo(g_ref, 0, dam, width - 1, exchanges + 1)
    for copy in sent:
        copy.start()
    pair(p_ref, 0).start()

    @pl.when(seg == 0)
    def _():
        cross(p_ref, 0).start()

    for load in loads:
        load.wait()

    zero = jnp.zeros(p_ref.shape[1:], jnp.float32)
    offset = jnp.where(seg == seg_n - 1, loc - shift_ref[0], loc)
    sums = []
    for column in range(KRY):
        source = p_ref if column == 0 else levels.at[STEPS, own]
        for part in range(STEPS // width):
            base = column * STEPS + part * width
            if base > 0:
                sent = halo(levels.at[base], width, levels.at[base], width, base // width)
                for copy in sent:
                    copy.start()
                if part == 0:
                    pair(source, column).start()

                    @pl.when(seg == 0)
                    def _():
                        cross(source, column).start()

            interior(base)
            for copy in sent:
                copy.wait()
            edges(base)
        pair(source, column).wait()

        @pl.when(seg == 0)
        def _():
            cross(source, column).wait_send()

        @pl.when(seg == seg_n - 1)
        def _():
            cross(source, column).wait_recv()

        last = (column + 1) * STEPS

        def couple(i, acc):
            image = levels[last, width + i] - coupled[column][offset + i]
            if column == 0:
                levels[last, width + i] = image
            first = levels[0, width + i]
            second = image if column == 0 else levels[STEPS, width + i]
            head = first * first if column == 0 else first * image
            mid = first * image if column == 0 else second * image
            return (acc[0] + head, acc[1] + mid, acc[2] + image * image)

        def couple_group(i, acc):
            for j in range(4):
                acc = couple(4 * i + j, acc)
            return acc

        sums += lax.fori_loop(0, loc // 4, couple_group, (zero, zero, zero))
        if column == 0:
            store = pltpu.make_async_copy(levels.at[STEPS, own], p1_ref, out_sem)
            store.start()

    lane = lax.broadcasted_iota(jnp.int32, (1, zero.shape[-1]), 1)
    row = jnp.zeros(lane.shape, jnp.float32)
    for place, entry in enumerate(sums):
        value = jnp.sum(jnp.sum(entry, axis=0), axis=(0, 1), keepdims=True)
        row = row + jnp.where(lane == place, value, 0.0)

    def share(row, buffer, me, count, where, send, recv):
        buffer[me] = row
        copies = []
        for d in range(1, count):
            copies.append(
                pltpu.make_async_remote_copy(
                    src_ref=buffer.at[me], dst_ref=buffer.at[me],
                    send_sem=send.at[d - 1], recv_sem=recv.at[d - 1],
                    device_id=where(d), device_id_type=MESH,
                )
            )
        for copy in copies:
            copy.start()
        for copy in copies:
            copy.wait()
        total = buffer[0]
        for d in range(1, count):
            total = total + buffer[d]
        return total

    row = share(row, seg_sums, seg, seg_n, lambda d: at(d, 0), seg_send, seg_recv)
    row = share(row, slab_sums, slab, slab_n, lambda d: at(0, d), slab_send, slab_recv)
    totals_ref[...] = row
    store.wait()


def step_kernel(radius_ref, totals_ref, p0_ref, p1_ref, step_ref, hess_ref, x0, x1, y, in_sem, out_sem):
    loc = p0_ref.shape[0]
    parts = 4
    size = loc // parts
    pieces = [pl.ds(i * size, size) for i in range(parts)]
    loads = []
    for i, piece in enumerate(pieces):
        loads.append(
            (
                pltpu.make_async_copy(p0_ref.at[piece], x0.at[piece], in_sem.at[0, i]),
                pltpu.make_async_copy(p1_ref.at[piece], x1.at[piece], in_sem.at[1, i]),
            )
        )
    for pair in loads:
        for load in pair:
            load.start()

    totals = totals_ref[...]
    lane = lax.broadcasted_iota(jnp.int32, totals.shape, 1)
    entry = lambda i: jnp.sum(jnp.where(lane == i, totals, 0.0), axis=1, keepdims=True)
    g00, g01, g11, g02, g12, g22 = [jnp.broadcast_to(entry(i), totals.shape) for i in range(6)]
    gram = ((g00, g01, g02), (g01, g11, g12), (g02, g12, g22))

    def form(left, right):
        total = None
        for i, a in left.items():
            inner = None
            for j, b in right.items():
                term = gram[i][j] * b
                inner = term if inner is None else inner + term
            total = a * inner if total is None else total + a * inner
        return total

    norm = jnp.sqrt(g00)
    v0 = {0: 1.0 / norm}
    image = {1: v0[0]}
    h00 = form(v0, image)
    image = {0: -h00 * v0[0], 1: image[1]}
    h10 = jnp.sqrt(form(image, image))
    v1 = {0: image[0] / h10, 1: image[1] / h10}
    image = {1: v1[0], 2: v1[1]}
    h01 = form(v0, image)
    h11 = form(v1, image)
    image = {0: -h01 * v0[0] - h11 * v1[0], 1: image[1] - h11 * v1[1], 2: image[2]}
    h21 = jnp.sqrt(form(image, image))

    radius = jnp.full(totals.shape, radius_ref[0], jnp.float32)
    ridge = 1.0 / (radius * radius)
    n00 = h00 * h00 + h10 * h10 + ridge
    n01 = h00 * h01 + h10 * h11
    n11 = h01 * h01 + h11 * h11 + h21 * h21 + ridge
    f00 = jnp.sqrt(n00)
    f10 = n01 / f00
    f11 = jnp.sqrt(n11 - f10 * f10)
    r0 = norm * h00 / f00
    r1 = (norm * h01 - f10 * r0) / f11
    w1 = r1 / f11
    w0 = (r0 - f10 * w1) / f00
    m0 = w0 * v0[0] + w1 * v1[0]
    m1 = w1 * v1[1]

    shape = hess_ref.shape
    i = lax.broadcasted_iota(jnp.int32, shape, 0)
    j = lax.broadcasted_iota(jnp.int32, shape, 1)
    hess = jnp.zeros(shape, jnp.float32)
    for r, c, value in ((0, 0, h00), (1, 0, h10), (0, 1, h01), (1, 1, h11), (2, 1, h21)):
        hess = jnp.where((i == r) & (j == c), value[:, : shape[1]], hess)
    hess_ref[...] = hess

    stores = []
    for n, piece in enumerate(pieces):
        for load in loads[n]:
            load.wait()
        y[piece] = m0 * x0[piece] + m1 * x1[piece]
        store = pltpu.make_async_copy(y.at[piece], step_ref.at[piece], out_sem.at[n])
        store.start()
        stores.append(store)
    for store in stores:
        store.wait()


def local(seg_n, slab_n, mismatch, advect, damping, axial_shift, radius):
    one, loc, rows, lanes = mismatch.shape
    shape = (loc, rows // 8, 8, lanes)
    width = WIDTH
    full = loc + 2 * width
    p, a, g = (x.reshape(shape) for x in (mismatch, advect, damping))
    plane = shape[1:]
    exchanges = KRY * STEPS // width
    dma = pltpu.SemaphoreType.DMA
    anywhere = pl.BlockSpec(memory_space=pl.ANY)
    smem = pl.BlockSpec(memory_space=pltpu.SMEM)
    vmem = pl.BlockSpec(memory_space=pltpu.VMEM)
    f32 = jnp.float32
    p1, totals = pl.pallas_call(
        functools.partial(krylov_kernel, seg_n, slab_n, width),
        out_shape=(jax.ShapeDtypeStruct(shape, f32), jax.ShapeDtypeStruct((1, lanes), f32)),
        in_specs=[smem, anywhere, anywhere, anywhere],
        out_specs=(anywhere, vmem),
        scratch_shapes=[
            pltpu.VMEM((KRY * STEPS + 1, full) + plane, f32),
            pltpu.VMEM((full,) + plane, f32),
            pltpu.VMEM((full,) + plane, f32),
            pltpu.VMEM((2 * loc,) + plane, f32),
            pltpu.VMEM((2 * loc,) + plane, f32),
            pltpu.VMEM((seg_n, 1, lanes), f32),
            pltpu.VMEM((slab_n, 1, lanes), f32),
            dma((3,)),
            dma((exchanges + 2, 2)),
            dma((exchanges + 2, 2)),
            dma((KRY,)),
            dma((KRY,)),
            dma((KRY,)),
            dma((KRY,)),
            dma,
            dma((seg_n - 1,)),
            dma((seg_n - 1,)),
            dma((slab_n - 1,)),
            dma((slab_n - 1,)),
        ],
        compiler_params=pltpu.CompilerParams(
            collective_id=0, has_side_effects=True, vmem_limit_bytes=32 * 2**20
        ),
        name="krylov",
    )(axial_shift, p, a, g)
    step, hessenberg = pl.pallas_call(
        step_kernel,
        out_shape=(jax.ShapeDtypeStruct(shape, f32), jax.ShapeDtypeStruct((KRY + 1, KRY), f32)),
        in_specs=[smem, vmem, anywhere, anywhere],
        out_specs=(anywhere, vmem),
        scratch_shapes=[
            pltpu.VMEM(shape, f32),
            pltpu.VMEM(shape, f32),
            pltpu.VMEM(shape, f32),
            dma((2, 4)),
            dma((4,)),
        ],
        compiler_params=pltpu.CompilerParams(vmem_limit_bytes=16 * 2**20),
        name="hookstep",
    )(radius, totals, p, p1)
    return step.reshape(mismatch.shape), hessenberg


def solution(mesh):
    field = P("seg", "slab", None, None)
    return jax.shard_map(
        functools.partial(local, mesh.shape["seg"], mesh.shape["slab"]),
        mesh=mesh,
        in_specs=(field, field, field, P(), P()),
        out_specs=(field, P()),
        check_vma=False,
    )
```

time: 202 us -> 56.9 us (0.28)
  waiting for transfers between devices: 68.5 us -> 0 us
  Pallas kernels: 0 us -> 50.9 us
  starting transfers between devices: 39.7 us -> 0 us
  blocking collectives: 37.1 us -> 0 us
  other arithmetic: 21.7 us -> 0 us
  local copies, waits for them, and re-layouts: 18.9 us -> 3.77 us
  between operations: 9.64 us -> 1.95 us
  matrix products: 4.53 us -> 0 us
    ppermute x36 -> x0, waiting for transfers between devices: 68.5 us -> none  [the longest x16 31.2 us: with_halo(): lax.ppermute(tail, axis, [(i, (i + 1) % count) for i in range(count)])]
    pallas_call x0 -> x2, Pallas kernels: none -> 50.9 us  [the longest x1 48.5 us: local(): pl.pallas_call(functools.partial(krylov_kernel, seg_n, slab_n, width), ou...]
    ppermute x36 -> x0, starting transfers between devices: 39.7 us -> none  [the longest x16 28 us: with_halo(): lax.ppermute(tail, axis, [(i, (i + 1) % count) for i in range(count)])]
    psum x1 -> x0, blocking collectives: 37.1 us -> none  [local(): rhs_total = lax.psum(jnp.sum(mismatch * mismatch), ('seg', 'slab'))]
    slice x69 -> x0, local copies, waits for them, and re-layouts: 14.5 us -> none  [the longest x30 7.89 us: advance(): t_behind = jnp.roll(centre, 1, axis=-1)]
    sub x16 -> x0, other arithmetic: 12.5 us -> none  [the longest x14 9.84 us: advance(): centre + KAPPA * (z_ahead + z_behind + r_outer + r_inner + t_ahead + t_be...]
    dot_general x5 -> x0, matrix products: 4.53 us -> none  [the longest x4 4.4 us: quad_form(): jnp.dot(gram_matrix, right, precision=lax.Precision.HIGHEST)]
    another operation x7 -> x0, other arithmetic: 4.24 us -> none  [the longest x3 2.04 us: local(): hessenberg = jnp.stack(columns, axis=1)]
  transfers between devices with their start and end apart: 36 -> 0, of which waited for: 33 -> 0; matrix products, arithmetic and copies ran while one was open for 11% -> 0% of each run, Pallas kernels for 0% -> 0%
where the time goes in v1:
time: 56.9 us; the launch traced here: 56.7 us
  Pallas kernels  50.9 us (89%)
  local copies, waits for them, and re-layouts  3.77 us (7%)
  between operations  1.95 us (3%)
    pallas_call x1, Pallas kernels, local(): pl.pallas_call(functools.partial(krylov_kernel, seg_n, slab_n, width), ou...  48.5 us
    unnamed x7, local copies, waits for them, and re-layouts  3.77 us
    pallas_call x1, Pallas kernels, local(): pl.pallas_call(step_kernel, out_shape=(jax.ShapeDtypeStruct(shape, f32),...  2.42 us

profile of v1, /device:TPU:0, one launch (start us, length us, event | category | flops | bytes accessed | tf_op | source)
XLA Modules:
  0.0 56.7 jit_solution(5823596707575732342)
XLA Ops:
  1.9 0.0 copy-start
  1.9 1.0 %copy-done = f32[1,32,32,128]{3,2,1,0:T(8,128)S(1)} copy-done((f32[1,32,32,128]{3,2,1,0:T(8,128)S(1)}, f32[1,32,32,128]{3,2,1,0:T(8,128)}, u32[]{:S(2)}) %copy-start) | copy-done | bytes 524312
  3.0 0.0 copy-start.1
  3.0 1.0 %copy-done.1 = f32[1,32,32,128]{3,2,1,0:T(8,128)S(1)} copy-done((f32[1,32,32,128]{3,2,1,0:T(8,128)S(1)}, f32[1,32,32,128]{3,2,1,0:T(8,128)}, u32[]{:S(2)}) %copy-start.1) | copy-done | bytes 524312
  4.0 0.0 copy-start.2
  4.0 1.0 %copy-done.2 = f32[1,32,32,128]{3,2,1,0:T(8,128)S(1)} copy-done((f32[1,32,32,128]{3,2,1,0:T(8,128)S(1)}, f32[1,32,32,128]{3,2,1,0:T(8,128)}, u32[]{:S(2)}) %copy-start.2) | copy-done | bytes 524312
  5.0 48.5 %krylov.1 = (f32[32,4,8,128]{3,2,1,0:T(8,128)S(1)}, f32[1,128]{1,0:T(1,128)S(1)}) custom-call(s32[1]{0:T(128)S(6)} %copy.8.shift_ref, f32[32,4,8,128]{3,2,1,0:T(8,128)S(1)} %bitcast.4, f32[32,4,8,128]{3,2,1,0:T(8,128)S(1)} %bitcast.6, f32[32,4,8,128]{3,2,1,0:T(8,128)S(1)} %bitcast.7), custom_call_target="tpu_custom_call" | custom-call | tf_op jit(solution)/shard_map/krylov/pallas_call | solution.py:313
  53.6 2.4 %hookstep.1 = (f32[32,4,8,128]{3,2,1,0:T(8,128)}, f32[3,2]{1,0:T(4,128)S(1)}) custom-call(f32[1]{0:T(128)S(6)} %copy.9.radius_ref, f32[1,128]{1,0:T(1,128)S(1)} %get-tuple-element.6.totals_ref, f32[32,4,8,128]{3,2,1,0:T(8,128)S(1)} %bitcast.5, f32[32,4,8,128]{3,2,1,0:T(8,128)S(1)} %get-tuple-element.7.p1_ref), custom_call_target="tpu_custom_call" | custom-call | tf_op jit(solution)/shard_map/hookstep/pallas_call | solution.py:344
  56.0 0.6 %copy.7 = f32[3,2]{0,1:T(2,128)} copy(f32[3,2]{1,0:T(4,128)S(1)} %get-tuple-element.11) | data formatting | bytes 48
Async XLA Ops:
  1.9 1.0 %copy-start = (f32[1,32,32,128]{3,2,1,0:T(8,128)S(1)}, f32[1,32,32,128]{3,2,1,0:T(8,128)}, u32[]{:S(2)}) copy-start(f32[1,32,32,128]{3,2,1,0:T(8,128)} %param.5) | copy-start | bytes 1572868
  3.0 1.0 %copy-start.1 = (f32[1,32,32,128]{3,2,1,0:T(8,128)S(1)}, f32[1,32,32,128]{3,2,1,0:T(8,128)}, u32[]{:S(2)}) copy-start(f32[1,32,32,128]{3,2,1,0:T(8,128)} %param.6) | copy-start | bytes 1572868
  4.0 1.0 %copy-start.2 = (f32[1,32,32,128]{3,2,1,0:T(8,128)S(1)}, f32[1,32,32,128]{3,2,1,0:T(8,128)}, u32[]{:S(2)}) copy-start(f32[1,32,32,128]{3,2,1,0:T(8,128)} %param.7) | copy-start | bytes 1572868

commit v2 on v1

--- a/solution.py
+++ b/solution.py
@@ -10,34 +10,41 @@
 STEPS = 8
 KRY = 2
 KAPPA = 0.15
-WIDTH = 8
+WIDTH = 4
 
 MESH = pl.DeviceIdType.MESH
 
 
-def stencil(behind, centre, ahead, advect, damping):
-    blocks, rows, lanes = centre.shape
-    row = lax.broadcasted_iota(jnp.int32, centre.shape, 1)
-    wall = jnp.zeros((1, rows, lanes), jnp.float32)
-    around = pltpu.roll(centre, 1, 2) + pltpu.roll(centre, lanes - 1, 2)
-    down = pltpu.roll(centre, 1, 1)
-    up = pltpu.roll(centre, rows - 1, 1)
-    inner = jnp.where(row == 0, jnp.concatenate([wall, down[:-1]], axis=0), down)
-    outer = jnp.where(row == rows - 1, jnp.concatenate([up[1:], wall], axis=0), up)
-    total = (around + (inner + outer)) + (ahead + behind)
-    return centre * ((1.0 - 6.0 * KAPPA) - damping) + KAPPA * total + (0.5 * advect) * (behind - ahead)
+def rows_of(ref, *place):
+    groups = ref.shape[-2] // 8
+    return [ref[(*place, pl.ds(j, 8, groups))] for j in range(groups)]
+
+
+def stencil(behind, centre, ahead, drift, keep):
+    groups = len(centre)
+    lanes = centre[0].shape[-1]
+    row = lax.broadcasted_iota(jnp.int32, centre[0].shape, 0)
+    inner = [jnp.where(row == 0, 0.0, pltpu.roll(centre[-1], 1, 0))] + centre[:-1]
+    outer = centre[1:] + [jnp.where(row == 7, 0.0, pltpu.roll(centre[0], 7, 0))]
+    result = []
+    for j in range(groups):
+        around = pltpu.roll(centre[j], 1, 1) + pltpu.roll(centre[j], lanes - 1, 1)
+        total = (around + (inner[j] + outer[j])) + (ahead[j] + behind[j])
+        result.append(centre[j] * keep[j] + KAPPA * total + drift[j] * (behind[j] - ahead[j]))
+    return result
 
 
 def krylov_kernel(
     seg_n, slab_n, width,
     shift_ref, p_ref, a_ref, g_ref,
     p1_ref, totals_ref,
-    levels, adv, dam, next_a, next_b, seg_sums, slab_sums,
+    levels, adv, dam, next_a, next_b, relay, seg_sums, slab_sums,
     load_sem, halo_send, halo_recv, pair_send, pair_recv, cross_send, cross_recv,
     out_sem, seg_send, seg_recv, slab_send, slab_recv,
 ):
     loc = p_ref.shape[0]
     full = loc + 2 * width
+    half = loc // 2
     seg = lax.axis_index("seg")
     slab = lax.axis_index("slab")
     at = lambda s, z: {"seg": lax.rem(seg + s, seg_n), "slab": lax.rem(slab + z, slab_n)}
@@ -45,7 +52,6 @@
 
     barrier = pltpu.get_barrier_semaphore()
     peers = [(0, z) for z in range(1, slab_n)] + [(s, 0) for s in range(1, seg_n)]
-    peers += [(seg_n - 1, 1), (1, slab_n - 1)]
     for s, z in peers:
         pl.semaphore_signal(barrier, inc=1, device_id=at(s, z), device_id_type=MESH)
     own = pl.ds(width, loc)
@@ -74,28 +80,92 @@
         ]
 
     def pair(source, column):
+        return [
+            pltpu.make_async_remote_copy(
+                src_ref=source.at[pl.ds(part * half, half)],
+                dst_ref=coupled[column].at[pl.ds(loc + part * half, half)],
+                send_sem=pair_send.at[column, part], recv_sem=pair_recv.at[column, part],
+                device_id=at(seg_n - 1, 0), device_id_type=MESH,
+            )
+            for part in (1, 0)
+        ]
+
+    def behind_first(source, column):
         return pltpu.make_async_remote_copy(
-            src_ref=source, dst_ref=coupled[column].at[pl.ds(loc, loc)],
-            send_sem=pair_send.at[column], recv_sem=pair_recv.at[column],
+            src_ref=source.at[pl.ds(0, half)], dst_ref=relay.at[column],
+            send_sem=cross_send.at[column, 0], recv_sem=cross_recv.at[column, 0],
+            device_id=at(0, 1), device_id_type=MESH,
+        )
+
+    def first_to_last(column):
+        return pltpu.make_async_remote_copy(
+            src_ref=relay.at[column], dst_ref=coupled[column].at[pl.ds(0, half)],
+            send_sem=cross_send.at[column, 1], recv_sem=cross_recv.at[column, 1],
             device_id=at(seg_n - 1, 0), device_id_type=MESH,
         )
 
-    def cross(source, column):
+    def behind_last(column):
         return pltpu.make_async_remote_copy(
-            src_ref=source, dst_ref=coupled[column].at[pl.ds(0, loc)],
-            send_sem=cross_send.at[column], recv_sem=cross_recv.at[column],
-            device_id=at(seg_n - 1, 1), device_id_type=MESH,
+            src_ref=coupled[column].at[pl.ds(loc + half, half)],
+            dst_ref=coupled[column].at[pl.ds(half, half)],
+            send_sem=cross_send.at[column, 2], recv_sem=cross_recv.at[column, 2],
+            device_id=at(0, 1), device_id_type=MESH,
         )
 
+    def couple_start(source, column):
+        for copy in pair(source, column):
+            copy.start()
+
+        @pl.when(seg == 0)
+        def _():
+            behind_first(source, column).start()
+
+    def couple_relay(source, column):
+        @pl.when(seg == 0)
+        def _():
+            behind_first(source, column).wait()
+            first_to_last(column).start()
+
+        @pl.when(seg == seg_n - 1)
+        def _():
+            pair(source, column)[0].wait_recv()
+            behind_last(column).start()
+
+    def couple_wait(source, column):
+        high, low = pair(source, column)
+        high.wait_send()
+        low.wait()
+
+        @pl.when(seg < seg_n - 1)
+        def _():
+            high.wait_recv()
+
+        @pl.when(seg == 0)
+        def _():
+            first_to_last(column).wait_send()
+
+        @pl.when(seg == seg_n - 1)
+        def _():
+            first_to_last(column).wait_recv()
+            behind_last(column).wait()
+
     def sweep(level, start, count):
-        before = levels[level, start - 1]
-        here = levels[level, start]
+        groups = levels.shape[-2] // 8
+        before = rows_of(levels, level, start - 1)
+        here = rows_of(levels, level, start)
         for plane in range(count):
-            after = levels[level, start + plane + 1]
-            levels[level + 1, start + plane] = stencil(
-                before, here, after, adv[start + plane], dam[start + plane]
+            after = rows_of(levels, level, start + plane + 1)
+            result = stencil(
+                before, here, after, rows_of(adv, start + plane), rows_of(dam, start + plane)
             )
+            for j in range(groups):
+                levels[level + 1, start + plane, pl.ds(j, 8, groups)] = result[j]
             before, here = here, after
+
+    def prepare(start, count):
+        for plane in range(count):
+            adv[start + plane] = 0.5 * adv[start + plane]
+            dam[start + plane] = (1.0 - 6.0 * KAPPA) - dam[start + plane]
 
     thirds = -(-(loc - 2) // 3)
 
@@ -121,15 +191,16 @@
     sent += halo(g_ref, 0, dam, width - 1, exchanges + 1)
     for copy in sent:
         copy.start()
-    pair(p_ref, 0).start()
-
-    @pl.when(seg == 0)
-    def _():
-        cross(p_ref, 0).start()
+    couple_start(p_ref, 0)
 
     for load in loads:
         load.wait()
 
+    def prepare_group(i, carry):
+        prepare(width + 4 * i, 4)
+        return carry
+
+    lax.fori_loop(0, loc // 4, prepare_group, 0)
     zero = jnp.zeros(p_ref.shape[1:], jnp.float32)
     offset = jnp.where(seg == seg_n - 1, loc - shift_ref[0], loc)
     sums = []
@@ -142,26 +213,17 @@
                 for copy in sent:
                     copy.start()
                 if part == 0:
-                    pair(source, column).start()
-
-                    @pl.when(seg == 0)
-                    def _():
-                        cross(source, column).start()
-
+                    couple_start(source, column)
+            if part == 1:
+                couple_relay(source, column)
             interior(base)
             for copy in sent:
                 copy.wait()
+            if base == 0:
+                prepare(1, width - 1)
+                prepare(width + loc, width - 1)
             edges(base)
-        pair(source, column).wait()
-
-        @pl.when(seg == 0)
-        def _():
-            cross(source, column).wait_send()
-
-        @pl.when(seg == seg_n - 1)
-        def _():
-            cross(source, column).wait_recv()
-
+        couple_wait(source, column)
         last = (column + 1) * STEPS
 
         def couple(i, acc):
@@ -187,7 +249,7 @@
     lane = lax.broadcasted_iota(jnp.int32, (1, zero.shape[-1]), 1)
     row = jnp.zeros(lane.shape, jnp.float32)
     for place, entry in enumerate(sums):
-        value = jnp.sum(jnp.sum(entry, axis=0), axis=(0, 1), keepdims=True)
+        value = jnp.sum(entry, axis=(0, 1), keepdims=True)
         row = row + jnp.where(lane == place, value, 0.0)
 
     def share(row, buffer, me, count, where, send, recv):
@@ -278,8 +340,8 @@
     m1 = w1 * v1[1]
 
     shape = hess_ref.shape
-    i = lax.broadcasted_iota(jnp.int32, shape, 0)
-    j = lax.broadcasted_iota(jnp.int32, shape, 1)
+    i = lax.broadcasted_iota(jnp.int32, shape, 1)
+    j = lax.broadcasted_iota(jnp.int32, shape, 0)
     hess = jnp.zeros(shape, jnp.float32)
     for r, c, value in ((0, 0, h00), (1, 0, h10), (0, 1, h01), (1, 1, h11), (2, 1, h21)):
         hess = jnp.where((i == r) & (j == c), value[:, : shape[1]], hess)
@@ -299,7 +361,7 @@
 
 def local(seg_n, slab_n, mismatch, advect, damping, axial_shift, radius):
     one, loc, rows, lanes = mismatch.shape
-    shape = (loc, rows // 8, 8, lanes)
+    shape = (loc, rows, lanes)
     width = WIDTH
     full = loc + 2 * width
     p, a, g = (x.reshape(shape) for x in (mismatch, advect, damping))
@@ -321,15 +383,16 @@
             pltpu.VMEM((full,) + plane, f32),
             pltpu.VMEM((2 * loc,) + plane, f32),
             pltpu.VMEM((2 * loc,) + plane, f32),
+            pltpu.VMEM((KRY, loc // 2) + plane, f32),
             pltpu.VMEM((seg_n, 1, lanes), f32),
             pltpu.VMEM((slab_n, 1, lanes), f32),
             dma((3,)),
             dma((exchanges + 2, 2)),
             dma((exchanges + 2, 2)),
-            dma((KRY,)),
-            dma((KRY,)),
-            dma((KRY,)),
-            dma((KRY,)),
+            dma((KRY, 2)),
+            dma((KRY, 2)),
+            dma((KRY, 3)),
+            dma((KRY, 3)),
             dma,
             dma((seg_n - 1,)),
             dma((seg_n - 1,)),
@@ -337,13 +400,13 @@
             dma((slab_n - 1,)),
         ],
         compiler_params=pltpu.CompilerParams(
-            collective_id=0, has_side_effects=True, vmem_limit_bytes=32 * 2**20
+            collective_id=0, has_side_effects=True
         ),
         name="krylov",
     )(axial_shift, p, a, g)
     step, hessenberg = pl.pallas_call(
         step_kernel,
-        out_shape=(jax.ShapeDtypeStruct(shape, f32), jax.ShapeDtypeStruct((KRY + 1, KRY), f32)),
+        out_shape=(jax.ShapeDtypeStruct(shape, f32), jax.ShapeDtypeStruct((KRY, KRY + 1), f32)),
         in_specs=[smem, vmem, anywhere, anywhere],
         out_specs=(anywhere, vmem),
         scratch_shapes=[
@@ -353,10 +416,9 @@
             dma((2, 4)),
             dma((4,)),
         ],
-        compiler_params=pltpu.CompilerParams(vmem_limit_bytes=16 * 2**20),
         name="hookstep",
     )(radius, totals, p, p1)
-    return step.reshape(mismatch.shape), hessenberg
+    return step.reshape(mismatch.shape), hessenberg.T
 
 
 def solution(mesh):

time: 56.9 us -> 49.8 us (0.88)
  local copies, waits for them, and re-layouts: 3.77 us -> 0 us
  Pallas kernels: 50.9 us -> 47.7 us
    pallas_call x1, Pallas kernels: 48.5 us -> 44.4 us  [local(): pl.pallas_call(functools.partial(krylov_kernel, seg_n, slab_n, width), ou...]
    unnamed x7 -> x0, local copies, waits for them, and re-layouts: 3.77 us -> none
    pallas_call x1, Pallas kernels: 2.42 us -> 3.29 us  [local(): pl.pallas_call(step_kernel, out_shape=(jax.ShapeDtypeStruct(shape, f32),...]
where the time goes in v2:
time: 49.8 us; the launch traced here: 49.6 us
  Pallas kernels  47.7 us (96%)
  between operations  1.93 us (4%)
    pallas_call x1, Pallas kernels, local(): pl.pallas_call(functools.partial(krylov_kernel, seg_n, slab_n, width), ou...  44.4 us
    pallas_call x1, Pallas kernels, local(): pl.pallas_call(step_kernel, out_shape=(jax.ShapeDtypeStruct(shape, f32),...  3.29 us

profile of v2, /device:TPU:0, one launch (start us, length us, event | category | flops | bytes accessed | tf_op | source)
XLA Modules:
  0.0 49.6 jit_solution(17870098134905246533)
XLA Ops:
  1.9 44.4 %krylov.1 = (f32[32,32,128]{2,1,0:T(8,128)}, f32[1,128]{1,0:T(1,128)}) custom-call(s32[1]{0:T(128)S(6)} %copy.7.shift_ref, f32[32,32,128]{2,1,0:T(8,128)} %bitcast.5, f32[32,32,128]{2,1,0:T(8,128)} %bitcast.7, f32[32,32,128]{2,1,0:T(8,128)} %bitcast.8), custom_call_target="tpu_custom_call" | custom-call | tf_op jit(solution)/shard_map/krylov/pallas_call | solution.py:375
  46.3 3.3 %hookstep.1 = (f32[32,32,128]{2,1,0:T(8,128)}, f32[2,3]{1,0:T(2,128)}) custom-call(f32[1]{0:T(128)S(6)} %copy.8.radius_ref, f32[1,128]{1,0:T(1,128)} %get-tuple-element.6.totals_ref, f32[32,32,128]{2,1,0:T(8,128)} %bitcast.6, f32[32,32,128]{2,1,0:T(8,128)} %get-tuple-element.7.p1_ref), custom_call_target="tpu_custom_call" | custom-call | tf_op jit(solution)/shard_map/hookstep/pallas_call | solution.py:407
